TPU v7x, 32 devices: a whole 2x2x4 slice. The times are simulated.
32 devices in a mesh: rows: 8 (over z, y), grp: 4 (over x, core).
Axes of the slice: x: 2, y: 2, z: 4, core: 2. Of those that a mesh axis runs over, the one named last changes fastest.
Arguments:
- panel: float32 [8192, 256], P(('rows', 'grp')), may hold values from -6000 to 6000
- trailing: float32 [8192, 2048], P(('rows', 'grp')), may hold values from -6000 to 6000
Outputs:
- upper_panel: float32 [256, 256], replicated
- projection: float32 [256, 2048], replicated
- updated: float32 [8192, 2048], P(('rows', 'grp'))
- upper_next: float32 [256, 256], replicated
All inputs are finite; a program needn't handle non-finite values.
Results may differ from a plain program's by a relative error of at most 0.00019.
Values sent between devices are 32-bit elements; how exact they have to be, the bound alone decides.
A program may use at most 128 MiB of HBM per device.

v0:
```python
import jax
import jax.numpy as jnp
from jax import lax
from jax.sharding import PartitionSpec as P


def cross(left, right):
    return lax.dot_general(
        left,
        right,
        (((0,), (0,)), ((), ())),
        precision=lax.Precision.HIGHEST,
        preferred_element_type=jnp.float32,
    )


def product(left, right):
    return jnp.dot(left, right, precision=lax.Precision.HIGHEST, preferred_element_type=jnp.float32)


def lower_inverse(lower):
    order = lower.shape[0]
    result = jnp.zeros((order, order), jnp.float32)
    for index in range(order):
        unit = (jnp.arange(order) == index).astype(jnp.float32)
        new_row = (
            unit - jnp.dot(lower[index, :], result, precision=lax.Precision.HIGHEST)
        ) / lower[index, index]
        result = result.at[index, :].set(new_row)
    return result


def factor_pair(matrix):
    order = matrix.shape[0]
    if order <= 16 or order % 2 == 1:
        lower = jnp.zeros((order, order), jnp.float32)
        row_ids = jnp.arange(order)
        for index in range(order):
            column = matrix[:, index] - jnp.dot(
                lower, lower[index, :], precision=lax.Precision.HIGHEST
            )
            pivot = jnp.sqrt(column[index])
            lower = lower.at[:, index].set(jnp.where(row_ids >= index, column / pivot, 0.0))
        return (lower, lower_inverse(lower))
    middle = order // 2
    first_low, first_inv = factor_pair(matrix[:middle, :middle])
    below = product(matrix[middle:, :middle], first_inv.T)
    schur = matrix[middle:, middle:] - product(below, below.T)
    second_low, second_inv = factor_pair(schur)
    below_inv = -product(second_inv, product(below, first_inv))
    zeros_block = jnp.zeros((middle, order - middle), jnp.float32)
    lower = jnp.concatenate(
        [
            jnp.concatenate([first_low, zeros_block], axis=1),
            jnp.concatenate([below, second_low], axis=1),
        ],
        axis=0,
    )
    inverse = jnp.concatenate(
        [
            jnp.concatenate([first_inv, zeros_block], axis=1),
            jnp.concatenate([below_inv, second_inv], axis=1),
        ],
        axis=0,
    )
    return (lower, inverse)


def upper_of(matrix):
    return factor_pair(matrix)[0].T


def per_device(panel, trailing):
    inv_rows = 1.0 / (panel.shape[0] * lax.axis_size(("rows", "grp")))
    width = panel.shape[1]
    gram_panel, cross_terms, gram_head = lax.psum(
        (
            cross(panel, panel),
            cross(panel, trailing),
            cross(trailing[:, :width], trailing[:, :width]),
        ),
        ("rows", "grp"),
    )
    lower, lower_inv = factor_pair(gram_panel * inv_rows)
    upper_panel = lower.T
    inverse = lower_inv.T
    ortho_basis = product(panel, inverse)
    projection = cross(inverse, cross_terms) * inv_rows
    updated = trailing - product(ortho_basis, projection)
    head_proj = projection[:, :width]
    upper_next = upper_of(gram_head * inv_rows - cross(head_proj, head_proj))
    return (upper_panel, projection, updated, upper_next)


def solution(mesh):
    return jax.shard_map(
        per_device,
        mesh=mesh,
        in_specs=(P(("rows", "grp"), None), P(("rows", "grp"), None)),
        out_specs=(P(), P(), P(("rows", "grp"), None), P()),
        check_vma=False,
    )
```

profile of v0, /device:TPU:0, one launch (start us, length us, event | category | flops | bytes accessed | tf_op | source)
XLA Modules:
  0.0 1853.8 jit_solution(8966382655848866502)
XLA Ops:
  7.2 2.4 fusion.1984
  9.6 4.8 fusion.2984
  25.9 130.2 %all-reduce.122.cloned.1.call-done = (f32[256,256]{1,0:T(8,128)}, f32[256,2048]{1,0:T(8,128)}, f32[256,256]{1,0:T(8,128)}) async-done(((f32[256,256]{1,0:T(8,128)}, f32[256,2048]{1,0:T(8,128)}, f32[256,256]{1,0:T(8,128)}), (f32[256,256]{1,0:T(8,128)}, f32[256,2048]{1,0:T(8,128)}, f32[256,256]{1,0:T(8,128)})) %all-reduce.122.cloned.1.call-update) | async-done | bytes 2621456 | tf_op jit(solution)/shard_map/psum | solution.py:76
  198.2 1.5 fusion.985
  204.1 1.5 fusion.993
  207.0 1.5 fusion.997
  210.0 1.5 fusion.1001
  211.5 1.5 fusion.1003
  308.7 1.5 fusion.1051
  314.6 1.5 fusion.1059
  317.5 1.5 fusion.1063
  571.1 1.5 fusion.1215
  577.0 1.5 fusion.1223
  774.8 1.5 fusion.1335
  783.5 1.5 fusion.1347
  983.4 1.5 fusion.1463
  986.3 1.5 fusion.1467
  995.1 1.5 fusion.1479
  1003.9 1.9 convolution_multiply_fusion
  1196.8 1.5 fusion.1591
  1205.6 1.5 fusion.1603
  1214.4 1.5 fusion.1615
  1406.4 1.5 fusion.1719
  1415.2 1.5 fusion.1731
  1424.1 1.5 fusion.1743
  1615.9 1.5 fusion.1847
  1624.7 1.5 fusion.1859
  1633.6 1.5 fusion.1871
  1788.3 1.5 fusion.1951
  1789.8 1.5 fusion.1953
  1798.6 1.5 fusion.1965
  1840.4 4.9 convolution_subtract_fusion
  (4283 shorter events, 1312.7 us)
Async XLA Ops:
  7.2 2.5 copy-start
  7.2 148.9 %all-reduce.122.cloned.1.call-start = ((), (), s32[]{:S(2)}) async-start(), calls=%async_computation | async-start | bytes 5242880 | tf_op jit(solution)/shard_map/psum | solution.py:76
  157.6 1578.2 %copy-start.35 = (f32[16]{0:T(128)}, f32[16]{0:T(128)S(1)}, u32[]{:S(2)}) copy-start(f32[16]{0:T(128)S(1)} %get-tuple-element.13089) | copy-start | bytes 196
  192.9 2.3 copy-start.8
  325.1 52.1 %copy-start.24 = (f32[16,16]{1,0:T(8,128)}, f32[16,16]{1,0:T(8,128)S(1)}, u32[]{:S(2)}) copy-start(f32[16,16]{1,0:T(8,128)S(1)} %fusion.2173) | copy-start | bytes 3076
  561.5 2.3 copy-start.4
  734.8 59.3 %copy-start.26 = (f32[16,16]{1,0:T(8,128)}, f32[16,16]{1,0:T(8,128)S(1)}, u32[]{:S(2)}) copy-start(f32[16,16]{1,0:T(8,128)S(1)} %fusion.2165) | copy-start | bytes 3076
  893.9 110.0 %copy-start.20 = (f32[256,2048]{1,0:T(8,128)S(1)}, f32[256,2048]{1,0:T(8,128)}, u32[]{:S(2)}) copy-start(f32[256,2048]{1,0:T(8,128)} %get-tuple-element.12621) | copy-start | bytes 6291460
  943.6 62.3 %copy-start.22 = (f32[16,16]{1,0:T(8,128)}, f32[16,16]{1,0:T(8,128)S(1)}, u32[]{:S(2)}) copy-start(f32[16,16]{1,0:T(8,128)S(1)} %fusion.2161) | copy-start | bytes 3076
  1003.9 3.3 copy-start.21
  1156.9 59.4 %copy-start.28 = (f32[16,16]{1,0:T(8,128)}, f32[16,16]{1,0:T(8,128)S(1)}, u32[]{:S(2)}) copy-start(f32[16,16]{1,0:T(8,128)S(1)} %fusion.2157) | copy-start | bytes 3076
  1575.8 59.4 %copy-start.29 = (f32[16,16]{1,0:T(8,128)}, f32[16,16]{1,0:T(8,128)S(1)}, u32[]{:S(2)}) copy-start(f32[16,16]{1,0:T(8,128)S(1)} %fusion.2149) | copy-start | bytes 3076
  1612.2 2.3 copy-start.16
  1695.9 79.1 %copy-start.9 = (f32[16,16]{1,0:T(8,128)S(1)}, f32[16,16]{1,0:T(8,128)}, u32[]{:S(2)}) copy-start(f32[16,16]{1,0:T(8,128)} %copy-done.8) | copy-start | bytes 3076
  1752.9 84.1 %copy-start.15 = (f32[16,16]{1,0:T(8,128)S(1)}, f32[16,16]{1,0:T(8,128)}, u32[]{:S(2)}) copy-start(f32[16,16]{1,0:T(8,128)} %copy-done.14) | copy-start | bytes 3076
  1756.7 81.2 %copy-start.17 = (f32[16,16]{1,0:T(8,128)S(1)}, f32[16,16]{1,0:T(8,128)}, u32[]{:S(2)}) copy-start(f32[16,16]{1,0:T(8,128)} %copy-done.16) | copy-start | bytes 3076
  1759.1 79.5 %copy-start.7 = (f32[16,16]{1,0:T(8,128)S(1)}, f32[16,16]{1,0:T(8,128)}, u32[]{:S(2)}) copy-start(f32[16,16]{1,0:T(8,128)} %copy-done.6) | copy-start | bytes 3076
  1772.5 29.9 %copy-start.36 = (f32[16]{0:T(128)S(1)}, f32[16]{0:T(128)}, u32[]{:S(2)}) copy-start(f32[16]{0:T(128)} %copy-done.35) | copy-start | bytes 196
  1773.8 64.8 %copy-start.30 = (f32[32,32]{1,0:T(8,128)S(1)}, f32[32,32]{1,0:T(8,128)}, u32[]{:S(2)}) copy-start(f32[32,32]{1,0:T(8,128)} %select_maximum_fusion.23) | copy-start | bytes 12292
  1774.6 65.8 %copy-start.18 = (f32[256,2048]{1,0:T(8,128)S(1)}, f32[256,2048]{1,0:T(8,128)}, u32[]{:S(2)}) copy-start(f32[256,2048]{1,0:T(8,128)} %param.2019) | copy-start | bytes 6291460
  1775.0 62.8 %copy-start.34 = (f32[32,32]{1,0:T(8,128)S(1)}, f32[32,32]{1,0:T(8,128)}, u32[]{:S(2)}) copy-start(f32[32,32]{1,0:T(8,128)} %select_maximum_fusion.21) | copy-start | bytes 12292
  1776.6 62.2 %copy-start.31 = (f32[32,32]{1,0:T(8,128)S(1)}, f32[32,32]{1,0:T(8,128)}, u32[]{:S(2)}) copy-start(f32[32,32]{1,0:T(8,128)} %select_maximum_fusion.19) | copy-start | bytes 12292
  1778.8 2.3 copy-start.3
  1840.3 4.9 copy-start.11
  1840.3 4.9 copy-start.25
  1840.4 4.9 copy-start.32
  1840.4 5.0 copy-start.13
  1840.4 5.0 copy-start.27
  1840.4 5.0 copy-start.33
  1840.4 5.1 copy-start.5
  1840.4 5.2 copy-start.2
  1840.4 5.2 copy-start.23
  (6 other events, 12.5 us)
Sparse Core Ops, SparseCore 0:
  15.8 140.1 all-reduce.121
where the time goes:
time: 1880 us; the launch traced here: 1850 us
  matrix products  562 us (30%)
  local copies, waits for them, and re-layouts  450 us (24%)
  between operations  356 us (19%)
  other arithmetic  355 us (19%)
  waiting for transfers between devices  130 us (7%)
    dot_general x496, matrix products, lower_inverse(): jnp.dot(lower[index, :], result, precision=lax.Precision.HIGHEST)  465 us
    another operation x943, other arithmetic  345 us
    slice x480, local copies, waits for them, and re-layouts, factor_pair(): pivot = jnp.sqrt(column[index])  288 us
    psum x1, waiting for transfers between devices, per_device(): lax.psum((cross(panel, panel), cross(panel, trailing), cross(trailing[:,...  130 us
    dot_general x481, matrix products, factor_pair(): jnp.dot(lower, lower[index, :], precision=lax.Precision.HIGHEST)  63.9 us
    scatter x512, local copies, waits for them, and re-layouts, factor_pair(): lower.at[:, index].set(jnp.where(row_ids >= index, column / pivot, 0.0))  43.8 us
    another operation x512, local copies, waits for them, and re-layouts  43.5 us
    slice x62, local copies, waits for them, and re-layouts, lower_inverse(): lower[index, index]  41.8 us

commit v1 on v0

v1 whole, which is shorter than its diff:
```python
import functools

import jax
import jax.numpy as jnp
from jax import lax
from jax.experimental import pallas as pl
from jax.experimental.pallas import tpu as pltpu
from jax.sharding import PartitionSpec as P

LANES = 128
GROUP = 8


def cross(left, right):
    return lax.dot_general(
        left,
        right,
        (((0,), (0,)), ((), ())),
        precision=lax.Precision.HIGHEST,
        preferred_element_type=jnp.float32,
    )


def product(left, right):
    return jnp.dot(left, right, precision=lax.Precision.HIGHEST, preferred_element_type=jnp.float32)


def eliminate(work, order, block, with_inverse):
    chunks = order // LANES
    for start in range(0, order, block):
        stop = start + block
        live = [v for v in range(chunks) if (v + 1) * LANES > start]
        if with_inverse:
            live += [chunks + v for v in range(chunks) if v * LANES < stop]
        parts = {v: work[start:stop, v * LANES : (v + 1) * LANES] for v in live}
        done = {v: [] for v in live}
        for base in range(start, stop, GROUP):
            count = stop - base
            row_ids = lax.broadcasted_iota(jnp.int32, (count, LANES), 0)
            home, offset = divmod(base, LANES)
            cols = [
                jnp.broadcast_to(parts[home][:, offset + c : offset + c + 1], (count, LANES))
                for c in range(GROUP)
            ]
            pivots = jnp.ones((GROUP, LANES), jnp.float32)
            for k in range(GROUP):
                pivot = cols[k][k : k + 1, :]
                pivots = jnp.where(row_ids[:GROUP] == k, pivot, pivots)
                mult = jnp.where(row_ids > k, cols[k] * (1.0 / pivot), 0.0)
                for c in range(k + 1, GROUP):
                    cols[c] = cols[c] - mult * cols[c][k : k + 1, :]
                for v in live:
                    parts[v] = parts[v] - mult * parts[v][k : k + 1, :]
            scale = lax.rsqrt(pivots)
            scale = scale * (1.5 - 0.5 * pivots * scale * scale)
            for v in live:
                done[v].append(parts[v][:GROUP] * scale)
                parts[v] = parts[v][GROUP:]
        for v in live:
            work[start:stop, v * LANES : (v + 1) * LANES] = jnp.concatenate(done[v], axis=0)
        if stop < order:
            low = (stop // LANES) * LANES
            left = work[start:stop, low:order]
            high = order + (-(-stop // LANES)) * LANES if with_inverse else order
            change = cross(left, work[start:stop, low:high])
            work[stop:order, low:high] = work[stop:order, low:high] - change[stop - low :]


def eye_block(order):
    rows = lax.broadcasted_iota(jnp.int32, (order, order), 0)
    cols = lax.broadcasted_iota(jnp.int32, (order, order), 1)
    return rows, cols


def factor_kernel(with_inverse, block, matrix_ref, upper_ref, *rest):
    order = matrix_ref.shape[0]
    work = rest[-1]
    rows, cols = eye_block(order)
    work[:, :order] = matrix_ref[...]
    if with_inverse:
        work[:, order:] = jnp.where(rows == cols, 1.0, 0.0)
    eliminate(work, order, block, with_inverse)
    upper_ref[...] = jnp.where(cols >= rows, work[:, :order], 0.0)
    if with_inverse:
        rest[0][...] = jnp.where(cols <= rows, work[:, order:], 0.0)


def factor(matrix, with_inverse, block=32):
    order = matrix.shape[0]
    shape = jax.ShapeDtypeStruct((order, order), jnp.float32)
    return pl.pallas_call(
        functools.partial(factor_kernel, with_inverse, block),
        out_shape=(shape,) * (1 + with_inverse),
        in_specs=[pl.BlockSpec(memory_space=pltpu.VMEM)],
        out_specs=(pl.BlockSpec(memory_space=pltpu.VMEM),) * (1 + with_inverse),
        scratch_shapes=[pltpu.VMEM((order, order * (1 + with_inverse)), jnp.float32)],
        name="factor",
    )(matrix)


def per_device(panel, trailing):
    inv_rows = 1.0 / (panel.shape[0] * lax.axis_size(("rows", "grp")))
    width = panel.shape[1]
    gram_panel, cross_terms, gram_head = lax.psum(
        (
            cross(panel, panel),
            cross(panel, trailing),
            cross(trailing[:, :width], trailing[:, :width]),
        ),
        ("rows", "grp"),
    )
    upper_panel, lower_inv = factor(gram_panel * inv_rows, True)
    ortho_basis = product(panel, lower_inv.T)
    projection = product(lower_inv, cross_terms) * inv_rows
    updated = trailing - product(ortho_basis, projection)
    head_proj = projection[:, :width]
    (upper_next,) = factor(gram_head * inv_rows - cross(head_proj, head_proj), False)
    return (upper_panel, projection, updated, upper_next)


def solution(mesh):
    return jax.shard_map(
        per_device,
        mesh=mesh,
        in_specs=(P(("rows", "grp"), None), P(("rows", "grp"), None)),
        out_specs=(P(), P(), P(("rows", "grp"), None), P()),
        check_vma=False,
    )
```

time: 1880 us -> 200 us (0.11); the launches traced: 1850 us -> 200 us
  matrix products: 562 us -> 19.6 us
  local copies, waits for them, and re-layouts: 450 us -> 2.23 us
  other arithmetic: 355 us -> 1.67 us
  between operations: 356 us -> 14.1 us
  Pallas kernels: 0 us -> 21.9 us
    dot_general x977 -> x0, matrix products: 529 us -> none  [the longest x496 465 us: lower_inverse(): jnp.dot(lower[index, :], result, precision=lax.Precision.HIGHEST)]
    slice x574 -> x0, local copies, waits for them, and re-layouts: 346 us -> none  [the longest x480 288 us: factor_pair(): pivot = jnp.sqrt(column[index])]
    another operation x943 -> x0, other arithmetic: 345 us -> none
    scatter x1008 -> x0, local copies, waits for them, and re-layouts: 57.8 us -> none  [the longest x512 43.8 us: factor_pair(): lower.at[:, index].set(jnp.where(row_ids >= index, column / pivot, 0.0))]
    another operation x512 -> x0, local copies, waits for them, and re-layouts: 43.5 us -> none
    pallas_call x0 -> x2, Pallas kernels: none -> 21.9 us  [factor(): pl.pallas_call(functools.partial(factor_kernel, with_inverse, block), out...]
where the time goes in v1:
time: 200 us
  waiting for transfers between devices  140 us (70%)
  Pallas kernels  21.9 us (11%)
  matrix products  19.6 us (10%)
  between operations  14.1 us (7%)
  local copies, waits for them, and re-layouts  2.23 us (1%)
    psum x1, waiting for transfers between devices, per_device(): lax.psum((cross(panel, panel), cross(panel, trailing), cross(trailing[:,...  140 us
    pallas_call x2, Pallas kernels, factor(): pl.pallas_call(functools.partial(factor_kernel, with_inverse, block), out...  21.9 us
    dot_general x3, matrix products, product(): jnp.dot(left, right, precision=lax.Precision.HIGHEST, preferred_element_t...  9.86 us
    dot_general x4, matrix products, cross(): lax.dot_general(left, right, (((0,), (0,)), ((), ())), precision=lax.Prec...  9.72 us
  transfers between devices with their start and end apart: 1, of which 1 were waited for; matrix products, arithmetic and copies ran while one was open for 0% of the time, Pallas kernels for 0%

profile of v1, /device:TPU:0, one launch (start us, length us, event | category | flops | bytes accessed | tf_op | source)
XLA Modules:
  0.0 199.8 jit_solution(11583023221063362957)
XLA Ops:
  7.2 0.0 copy-start
  7.2 0.0 all-reduce.3.cloned.1.call-start
  7.2 0.9 copy-done
  8.1 1.3 fusion.3
  9.4 2.3 %fusion.1 = f32[256,256]{1,0:T(8,128)} fusion(f32[256,2048]{1,0:T(8,128)} %param.3), kind=kOutput, calls=%fused_computation.4 | convolution fusion | flops 201326592 | bytes 524288 | tf_op jit(solution)/shard_map/dot_general | solution.py:15
  11.7 4.8 %fusion.4 = f32[256,2048]{1,0:T(8,128)} fusion(f32[256,256]{1,0:T(8,128)S(1)} %copy-done, f32[256,2048]{1,0:T(8,128)} %param.3), kind=kOutput, calls=%fused_computation.8 | convolution fusion | flops 1610612736 | bytes 4456448 | tf_op jit(solution)/shard_map/dot_general | solution.py:15
  16.5 0.0 all-reduce.3.cloned.1.call-update
  16.6 140.3 %all-reduce.3.cloned.1.call-done = (f32[256,256]{1,0:T(8,128)}, f32[256,2048]{1,0:T(8,128)}, f32[256,256]{1,0:T(8,128)}) async-done(((f32[256,256]{1,0:T(8,128)}, f32[256,2048]{1,0:T(8,128)}, f32[256,256]{1,0:T(8,128)}), (f32[256,256]{1,0:T(8,128)}, f32[256,2048]{1,0:T(8,128)}, f32[256,256]{1,0:T(8,128)})) %all-reduce.3.cloned.1.call-update) | async-done | bytes 2621456 | tf_op jit(solution)/shard_map/psum | solution.py:104
  156.9 1.7 broadcast_multiply_fusion.matrix_ref
  158.5 11.1 %factor.2 = (f32[256,256]{1,0:T(8,128)}, f32[256,256]{1,0:T(8,128)}) custom-call(f32[256,256]{1,0:T(8,128)} %broadcast_multiply_fusion.matrix_ref), custom_call_target="tpu_custom_call" | custom-call | tf_op jit(solution)/shard_map/factor/pallas_call | solution.py:91
  169.6 1.4 fusion.5
  171.0 0.0 copy-start.3
  171.0 0.0 copy-start.1
  171.0 3.7 %convolution_multiply_fusion = f32[256,2048]{1,0:T(8,128)S(1)} fusion(f32[256,256]{1,0:T(8,128)} %get-tuple-element.7, f32[256,2048]{1,0:T(8,128)} %get-tuple-element.9), kind=kOutput, calls=%fused_computation.1 | convolution fusion | flops 1611137024 | bytes 4456448 | tf_op jit(solution)/shard_map/dot_general | solution.py:25
  174.7 0.0 copy-start.2
  174.7 1.3 copy-done.2
  176.0 0.0 copy-done.3
  176.0 1.3 convolution_subtract_fusion.1.matrix_ref
  177.3 10.8 %factor.3 = f32[256,256]{1,0:T(8,128)} custom-call(f32[256,256]{1,0:T(8,128)} %convolution_subtract_fusion.1.matrix_ref), custom_call_target="tpu_custom_call" | custom-call | tf_op jit(solution)/shard_map/factor/pallas_call | solution.py:91
  188.2 0.0 copy-done.1
  188.2 4.8 %convolution_subtract_fusion = f32[256,2048]{1,0:T(8,128)} fusion(f32[256,2048]{1,0:T(8,128)S(1)} %copy-done.1, f32[256,256]{1,0:T(8,128)S(1)} %fusion.5, f32[256,2048]{1,0:T(8,128)} %copy-done.2), kind=kOutput, calls=%fused_computation | convolution fusion | flops 1611137024 | bytes 6553600 | tf_op jit(solution)/shard_map/dot_general | solution.py:25
Async XLA Ops:
  7.2 1.0 copy-start
  7.2 149.7 %all-reduce.3.cloned.1.call-start = ((), (), s32[]{:S(2)}) async-start(), calls=%async_computation | async-start | bytes 5242880 | tf_op jit(solution)/shard_map/psum | solution.py:104
  171.0 5.1 %copy-start.3 = (f32[256,256]{1,0:T(8,128)S(1)}, f32[256,256]{1,0:T(8,128)}, u32[]{:S(2)}) copy-start(f32[256,256]{1,0:T(8,128)} %get-tuple-element.10) | copy-start | bytes 786436
  171.0 17.2 %copy-start.1 = (f32[256,2048]{1,0:T(8,128)S(1)}, f32[256,2048]{1,0:T(8,128)}, u32[]{:S(2)}) copy-start(f32[256,2048]{1,0:T(8,128)} %param.3) | copy-start | bytes 6291460
  174.7 1.3 copy-start.2
Sparse Core Ops, SparseCore 0:
  16.7 140.1 all-reduce.2

commit v2 on v1

--- a/solution.py
+++ b/solution.py
@@ -98,7 +98,229 @@
     )(matrix)
 
 
-def per_device(panel, trailing):
+def split(value):
+    high = value.astype(jnp.bfloat16)
+    return high, (value - high.astype(jnp.float32)).astype(jnp.bfloat16)
+
+
+def triple(left, right):
+    (a, b), (c, d) = left, right
+    dot = functools.partial(jnp.dot, preferred_element_type=jnp.float32)
+    return dot(a, c) + (dot(a, d) + dot(b, c))
+
+
+class Stream:
+    def __init__(self, lo, hi, axes, sizes, order):
+        self.cols = slice(lo, hi)
+        self.axes, self.sizes = axes, sizes
+        self.slab = order // sizes[0]
+        self.part = self.slab // sizes[1]
+        self.width = hi - lo
+
+    def scratch(self):
+        first, second = self.sizes
+        return [
+            pltpu.VMEM((first - 1, self.slab, self.width), jnp.float32),
+            pltpu.VMEM((self.slab, self.width), jnp.float32),
+            pltpu.VMEM((second - 1, self.part, self.width), jnp.float32),
+            pltpu.SemaphoreType.DMA((4, max(self.sizes))),
+            pltpu.SemaphoreType.DMA((4, max(self.sizes))),
+        ]
+
+    def bind(self, local, total, refs):
+        self.local, self.total = local, total
+        self.recv_first, self.sums, self.recv_second, self.send_sem, self.recv_sem = refs
+
+    def rows(self, index, size):
+        return pl.ds(pl.multiple_of(index * size, GROUP), size)
+
+    def own(self):
+        place = lax.axis_index(self.axes[0]) * self.sizes[1] + lax.axis_index(self.axes[1])
+        return self.rows(place, self.part)
+
+    def send(self, stage):
+        which = (0, 1, 1, 0)[stage]
+        axis, size = self.axes[which], self.sizes[which]
+        me = lax.axis_index(axis)
+        self.copies = []
+        for k in range(1, size):
+            peer = lax.rem(me + k, size)
+            if stage == 0:
+                src = self.local.at[self.rows(peer, self.slab), self.cols]
+                dst = self.recv_first.at[k - 1]
+            elif stage == 1:
+                src = self.sums.at[self.rows(peer, self.part), :]
+                dst = self.recv_second.at[k - 1]
+            else:
+                rows = self.own() if stage == 2 else self.rows(me, self.slab)
+                src = dst = self.total.at[rows, self.cols]
+            copy = pltpu.make_async_remote_copy(
+                src_ref=src,
+                dst_ref=dst,
+                send_sem=self.send_sem.at[stage, k - 1],
+                recv_sem=self.recv_sem.at[stage, k - 1],
+                device_id={axis: peer},
+                device_id_type=pl.DeviceIdType.MESH,
+            )
+            copy.start()
+            self.copies.append(copy)
+
+    def finish(self, stage):
+        for copy in self.copies:
+            copy.wait()
+        if stage == 0:
+            me = lax.axis_index(self.axes[0])
+            value = self.local[self.rows(me, self.slab), self.cols]
+            for k in range(self.sizes[0] - 1):
+                value = value + self.recv_first[k]
+            self.sums[...] = value
+        elif stage == 1:
+            me = lax.axis_index(self.axes[1])
+            value = self.sums[self.rows(me, self.part), :]
+            for k in range(self.sizes[1] - 1):
+                value = value + self.recv_second[k]
+            self.total[self.own(), self.cols] = value
+
+    def step(self, stage):
+        self.finish(stage)
+        self.send(stage + 1)
+
+
+def make_streams(order, width, rows, grp):
+    middle = 3 * order + (width - order) // 2 // LANES * LANES
+    return [
+        Stream(0, order, ("grp", "rows"), (grp, rows), order),
+        Stream(order, 3 * order, ("rows", "grp"), (rows, grp), order),
+        Stream(3 * order, middle, ("grp", "rows"), (grp, rows), order),
+        Stream(middle, 2 * order + width, ("rows", "grp"), (rows, grp), order),
+    ]
+
+
+def whole_kernel(rows, grp, panel_ref, trailing_ref, upper_ref, proj_ref, updated_ref, next_ref,
+                 local, total, work, high_ref, low_ref, *stream_refs):
+    order = panel_ref.shape[1]
+    width = trailing_ref.shape[1]
+    inv_rows = 1.0 / (panel_ref.shape[0] * rows * grp)
+    streams = make_streams(order, width, rows, grp)
+    for index, stream in enumerate(streams):
+        stream.bind(local, total, stream_refs[5 * index : 5 * index + 5])
+    gram, lead, left, right = streams
+
+    barrier = pltpu.get_barrier_semaphore()
+    for axis, size in (("rows", rows), ("grp", grp)):
+        me = lax.axis_index(axis)
+        for k in range(1, size):
+            pl.semaphore_signal(barrier, inc=1, device_id={axis: lax.rem(me + k, size)},
+                                device_id_type=pl.DeviceIdType.MESH)
+
+    panel = panel_ref[...]
+    head = trailing_ref[:, :order]
+    local[:, :order] = cross(panel, panel)
+    pl.semaphore_wait(barrier, rows + grp - 2)
+    gram.send(0)
+    local[:, order : 2 * order] = cross(head, head)
+    local[:, 2 * order : 3 * order] = cross(panel, head)
+    lead.send(0)
+    high, low = split(panel.T)
+    high_ref[...] = high
+    low_ref[...] = low
+
+    def cross_tiles(lo, hi):
+        @pl.loop(0, (hi - lo) // LANES)
+        def _(tile):
+            at = pl.multiple_of(lo + tile * LANES, LANES)
+            value = split(trailing_ref[:, pl.ds(at - 2 * order, LANES)])
+            local[:, pl.ds(at, LANES)] = triple((high_ref[...], low_ref[...]), value)
+
+    gram.step(0)
+    cross_tiles(left.cols.start, left.cols.stop)
+    left.send(0)
+    gram.step(1)
+    cross_tiles(right.cols.start, right.cols.stop)
+    right.send(0)
+    lead.step(0)
+    gram.step(2)
+    lead.step(1)
+    gram.finish(3)
+    lead.step(2)
+
+    ids, cols = eye_block(order)
+    work[:, :order] = total[:, :order] * inv_rows
+    work[:, order:] = jnp.where(ids == cols, 1.0, 0.0)
+    eliminate(work, order, 32, True)
+    upper_ref[...] = jnp.where(cols >= ids, work[:, :order], 0.0)
+    inverse = jnp.where(cols <= ids, work[:, order:], 0.0)
+    work[:, order:] = inverse
+
+    left.step(0)
+    right.step(0)
+    left.step(1)
+    right.step(1)
+    left.step(2)
+    right.step(2)
+    lead.finish(3)
+
+    head_proj = product(inverse, total[:, 2 * order : 3 * order]) * inv_rows
+    proj_ref[:, :order] = head_proj
+    work[:, :order] = total[:, order : 2 * order] * inv_rows - cross(head_proj, head_proj)
+    eliminate(work, order, 32, False)
+    next_ref[...] = jnp.where(cols >= ids, work[:, :order], 0.0)
+
+    basis = lax.dot_general(panel_ref[...], work[:, order:], (((1,), (1,)), ((), ())),
+                            precision=lax.Precision.HIGHEST,
+                            preferred_element_type=jnp.float32)
+    high, low = split(basis)
+    high_ref[...] = high
+    low_ref[...] = low
+    updated_ref[:, :order] = trailing_ref[:, :order] - triple((high, low), split(proj_ref[:, :order]))
+    left.finish(3)
+    right.finish(3)
+
+    @pl.loop(0, (width - order) // LANES)
+    def _(tile):
+        at = pl.multiple_of(order + tile * LANES, LANES)
+        here = pl.ds(at, LANES)
+        value = split(total[:, pl.ds(2 * order + at, LANES)] * inv_rows)
+        coeff = triple(split(work[:, order:]), value)
+        proj_ref[:, here] = coeff
+        change = triple((high_ref[...], low_ref[...]), split(coeff))
+        updated_ref[:, here] = trailing_ref[:, here] - change
+
+
+def fused(rows, grp, panel, trailing):
+    order = panel.shape[1]
+    width = trailing.shape[1]
+    streams = make_streams(order, width, rows, grp)
+    vmem = pl.BlockSpec(memory_space=pltpu.VMEM)
+    square = jax.ShapeDtypeStruct((order, order), jnp.float32)
+    scratch = [
+        pltpu.VMEM((order, 2 * order + width), jnp.float32),
+        pltpu.VMEM((order, 2 * order + width), jnp.float32),
+        pltpu.VMEM((order, 2 * order), jnp.float32),
+        pltpu.VMEM((order, panel.shape[0]), jnp.bfloat16),
+        pltpu.VMEM((order, panel.shape[0]), jnp.bfloat16),
+    ]
+    for stream in streams:
+        scratch += stream.scratch()
+    return pl.pallas_call(
+        functools.partial(whole_kernel, rows, grp),
+        out_shape=(
+            square,
+            jax.ShapeDtypeStruct((order, width), jnp.float32),
+            jax.ShapeDtypeStruct(trailing.shape, jnp.float32),
+            square,
+        ),
+        in_specs=[vmem, vmem],
+        out_specs=(vmem,) * 4,
+        scratch_shapes=scratch,
+        compiler_params=pltpu.CompilerParams(
+            collective_id=0, has_side_effects=True, vmem_limit_bytes=56 * 2**20
+        ),
+        name="panel_step",
+    )(panel, trailing)
+
+
+def plain(panel, trailing):
     inv_rows = 1.0 / (panel.shape[0] * lax.axis_size(("rows", "grp")))
     width = panel.shape[1]
     gram_panel, cross_terms, gram_head = lax.psum(
@@ -119,6 +341,16 @@
 
 
 def solution(mesh):
+    rows, grp = mesh.shape["rows"], mesh.shape["grp"]
+
+    def per_device(panel, trailing):
+        count, order = panel.shape
+        width = trailing.shape[1]
+        fits = order % (rows * grp * GROUP) == 0 and order % LANES == 0 and count == order
+        if fits and width % LANES == 0 and width >= 2 * order and min(rows, grp) > 1:
+            return fused(rows, grp, panel, trailing)
+        return plain(panel, trailing)
+
     return jax.shard_map(
         per_device,
         mesh=mesh,

time: 200 us -> 105 us (0.53)
  the two profiles are of different devices: /device:TPU:0 before, /device:TPU:15 now
where the time goes in v2:
time: 105 us; the launch traced here: 104 us
  Pallas kernels  96.8 us (92%)
  local copies, waits for them, and re-layouts  6.98 us (7%)
    pallas_call x1, Pallas kernels, fused(): pl.pallas_call(functools.partial(whole_kernel, rows, grp), out_shape=(squ...  96.8 us
    unnamed x8, local copies, waits for them, and re-layouts  6.98 us

profile of v2, /device:TPU:15, one launch (start us, length us, event | category | flops | bytes accessed | tf_op | source)
XLA Modules:
  0.0 104.5 jit_solution(7869483621022701356)
XLA Ops:
  0.6 96.8 %panel_step.1 = (f32[256,256]{1,0:T(8,128)}, f32[256,2048]{1,0:T(8,128)}, f32[256,2048]{1,0:T(8,128)}, f32[256,256]{1,0:T(8,128)}) custom-call(f32[256,256]{1,0:T(8,128)} %panel_ref.1, f32[256,2048]{1,0:T(8,128)} %trailing_ref.1), custom_call_target="tpu_custom_call" | custom-call | tf_op jit(solution)/shard_map/panel_step/pallas_call | solution.py:305
  97.5 1.7 %copy.10 = f32[256,256]{1,0:T(8,128)} copy(f32[256,256]{1,0:T(8,128)} %get-tuple-element.8) | data formatting | bytes 524288
  99.2 0.0 copy-start
  99.2 3.3 %copy.11 = f32[256,2048]{1,0:T(8,128)} copy(f32[256,2048]{1,0:T(8,128)} %get-tuple-element.9) | data formatting | bytes 4194304
  102.4 0.0 copy-done
  102.4 0.0 copy-start.1
  102.4 1.3 %copy.12 = f32[256,2048]{1,0:T(8,128)} copy(f32[256,2048]{1,0:T(8,128)S(1)} %copy-done) | data formatting | bytes 4194304
  103.8 0.0 copy-done.1
  103.8 0.7 copy.13
Async XLA Ops:
  99.2 3.3 %copy-start = (f32[256,2048]{1,0:T(8,128)S(1)}, f32[256,2048]{1,0:T(8,128)}, u32[]{:S(2)}) copy-start(f32[256,2048]{1,0:T(8,128)} %get-tuple-element.10) | copy-start | bytes 6291460
  102.4 1.3 %copy-start.1 = (f32[256,256]{1,0:T(8,128)S(1)}, f32[256,256]{1,0:T(8,128)}, u32[]{:S(2)}) copy-start(f32[256,256]{1,0:T(8,128)} %get-tuple-element.11) | copy-start | bytes 786436
